TPU v7x, 32 devices: a whole 2x2x4 slice. The times are simulated.
32 devices in a mesh: tok: 4 (over z), hid: 8 (over y, x, core).
Axes of the slice: x: 2, y: 2, z: 4, core: 2. Of those that a mesh axis runs over, the one named last changes fastest.
Arguments:
- tokens: bfloat16 [2048, 1024], P('tok', 'hid'), may hold values from -6 to 6
- cotangent: bfloat16 [2048, 1024], P('tok', 'hid'), may hold values from -6 to 6
- frozen_in: bfloat16 [1024, 16384], P('tok', 'hid'), may hold values from -0.1875 to 0.1875
- frozen_out: bfloat16 [16384, 1024], P('hid', 'tok'), may hold values from -0.046875 to 0.046875
- input_adapter_first: bfloat16 [1024, 128], P('hid'), may hold values from -0.1875 to 0.1875
- input_adapter_second: bfloat16 [128, 16384], P(None, 'hid'), may hold values from -0.5 to 0.5
- adapter_out_a: bfloat16 [16384, 128], P('hid'), may hold values from -0.046875 to 0.046875
- adapter_out_b: bfloat16 [128, 1024], replicated, may hold values from -0.5 to 0.5
Outputs:
- input_gradient: float32 [2048, 1024], P('tok', 'hid')
- grad_in_a: float32 [1024, 128], P('hid')
- grad_in_b: float32 [128, 16384], P(None, 'hid')
- grad_out_a: float32 [16384, 128], P('hid')
- grad_out_b: float32 [128, 1024], P(None, 'hid')
All inputs are finite; a program needn't handle non-finite values.
Results may differ from a plain program's by a relative error of at most 0.0029.
Values may be sent and summed in bfloat16 or wider, within the bound.
A program may use at most 64 MiB of HBM per device.

v0:
```python
import math
import jax
import jax.numpy as jnp
from jax import lax
from jax.sharding import PartitionSpec as P

ADAPTER_SCALE = 0.5
GELU_K = 0.7978845608
GELU_C = 0.044715


def gelu_pair(pre_activation):
    tangent = jnp.tanh(
        GELU_K * (pre_activation + GELU_C * pre_activation * pre_activation * pre_activation)
    )
    value_out = 0.5 * pre_activation * (1.0 + tangent)
    slopes = 0.5 * (1.0 + tangent) + 0.5 * pre_activation * (1.0 - tangent * tangent) * GELU_K * (
        1.0 + 3.0 * GELU_C * pre_activation * pre_activation
    )
    return (value_out, slopes)


def local(
    tokens,
    cotangent,
    frozen_in,
    frozen_out,
    input_adapter_first,
    input_adapter_second,
    adapter_out_a,
    adapter_out_b,
):
    highest_precision = lax.Precision.HIGHEST
    device_local_rows = tokens.shape[0]
    rank_width = input_adapter_second.shape[0]
    gradient_scale = ADAPTER_SCALE / math.sqrt(device_local_rows * lax.axis_size("tok"))
    full_tokens, full_cotan = (
        lax.all_gather(tokens, "hid", axis=1, tiled=True),
        lax.all_gather(cotangent, "hid", axis=1, tiled=True),
    )
    in_rows = lax.all_gather(frozen_in, "tok", axis=0, tiled=True)
    in_a_full = lax.all_gather(input_adapter_first, "hid", axis=0, tiled=True)
    lowrank_input = jnp.dot(full_tokens, in_a_full, preferred_element_type=jnp.float32)
    second_float = input_adapter_second.astype(jnp.float32)
    out_a_float = adapter_out_a.astype(jnp.float32)
    pre_activation = jnp.dot(
        full_tokens, in_rows, preferred_element_type=jnp.float32
    ) + ADAPTER_SCALE * jnp.dot(lowrank_input, second_float, precision=highest_precision)
    value_out, slopes = gelu_pair(pre_activation)
    hidden_act = value_out.astype(jnp.bfloat16)
    backward_lowrank = jnp.einsum(
        "td,rd->tr", full_cotan, adapter_out_b, preferred_element_type=jnp.float32
    )
    rank_out = jnp.dot(hidden_act, adapter_out_a, preferred_element_type=jnp.float32)
    dense_backward = jnp.einsum(
        "td,fd->tf",
        full_cotan,
        lax.all_gather(frozen_out, "tok", axis=1, tiled=True),
        preferred_element_type=jnp.float32,
    )
    dense_backward = dense_backward + ADAPTER_SCALE * jnp.dot(
        backward_lowrank, out_a_float.T, precision=highest_precision
    )
    grad_pre = (dense_backward * slopes).astype(jnp.bfloat16)
    rank_backward = jnp.einsum(
        "tf,rf->tr", grad_pre, input_adapter_second, preferred_element_type=jnp.float32
    )
    dense_in = jnp.einsum("tf,df->td", grad_pre, in_rows, preferred_element_type=jnp.float32)
    grad_out_a = gradient_scale * jnp.dot(
        hidden_act.astype(jnp.float32).T, backward_lowrank, precision=highest_precision
    )
    grad_in_b = gradient_scale * jnp.dot(
        lowrank_input.T, grad_pre.astype(jnp.float32), precision=highest_precision
    )
    in_a_float = in_a_full.astype(jnp.float32)
    dx_term = dense_in + ADAPTER_SCALE * jnp.dot(
        rank_backward, in_a_float.T, precision=highest_precision
    )
    out_term = jnp.dot(rank_out.T, full_cotan.astype(jnp.float32), precision=highest_precision)
    in_term = jnp.dot(rank_backward.T, full_tokens.astype(jnp.float32), precision=highest_precision)
    rank_terms = jnp.concatenate([out_term, in_term], axis=0)
    input_gradient, rank_local = (
        lax.psum_scatter(dx_term, "hid", scatter_dimension=1, tiled=True),
        lax.psum_scatter(rank_terms, "hid", scatter_dimension=1, tiled=True),
    )
    grad_out_a, grad_in_b, rank_total = lax.psum((grad_out_a, grad_in_b, rank_local), "tok")
    grad_out_b = gradient_scale * rank_total[:rank_width]
    grad_in_a = gradient_scale * rank_total[rank_width:].T
    return (input_gradient, grad_in_a, grad_in_b, grad_out_a, grad_out_b)


def solution(mesh):
    in_specs = (
        P("tok", "hid"),
        P("tok", "hid"),
        P("tok", "hid"),
        P("hid", "tok"),
        P("hid", None),
        P(None, "hid"),
        P("hid", None),
        P(),
    )
    out_specs = (P("tok", "hid"), P("hid", None), P(None, "hid"), P("hid", None), P(None, "hid"))
    return jax.shard_map(local, mesh=mesh, in_specs=in_specs, out_specs=out_specs, check_vma=False)
```

profile of v0, /device:TPU:0, one launch (start us, length us, event | category | flops | bytes accessed | tf_op | source)
XLA Modules:
  0.0 421.3 jit_solution(1950593718763780741)
XLA Ops:
  7.2 0.7 all-gather.5.cloned.1.call-update
  8.0 0.7 all-gather.9.cloned.1.call-update
  8.7 0.7 all-gather.11.cloned.1.call-update
  9.4 0.5 all-gather.7.cloned.1.call-update
  10.0 11.0 %all_gather.19 = bf16[1024,128]{1,0:T(8,128)(2,1)S(1)} all-gather(bf16[128,128]{1,0:T(8,128)(2,1)} %param.12), channel_id=1, replica_groups=mesh['tok'=4,'hid'=8] {'hid'}, dimensions={0}, use_global_device_ids=true | all-gather | bytes 294912 | tf_op jit(solution)/shard_map/all_gather | solution.py:42
  21.0 15.1 %all-gather.5.cloned.1.call-done = bf16[512,1024]{1,0:T(8,128)(2,1)} async-done(((bf16[512,128]{1,0:T(8,128)(2,1)}), bf16[512,1024]{1,0:T(8,128)(2,1)}) %all-gather.5.cloned.1.call-update) | async-done | bytes 1048592 | tf_op jit(solution)/shard_map/all_gather | solution.py:39
  36.1 1.7 fusion.9
  37.8 23.7 %all-gather.9.cloned.1.call-done = bf16[512,1024]{1,0:T(8,128)(2,1)} async-done(((bf16[512,128]{1,0:T(8,128)(2,1)}), bf16[512,1024]{1,0:T(8,128)(2,1)}) %all-gather.9.cloned.1.call-update) | async-done | bytes 1048592 | tf_op jit(solution)/shard_map/all_gather | solution.py:38
  61.5 1.7 fusion.11
  63.2 80.7 %all-gather.11.cloned.1.call-done = bf16[1024,2048]{1,0:T(8,128)(2,1)} async-done(((bf16[256,2048]{1,0:T(8,128)(2,1)}), bf16[1024,2048]{1,0:T(8,128)(2,1)}) %all-gather.11.cloned.1.call-update) | async-done | bytes 4194320 | tf_op jit(solution)/shard_map/all_gather | solution.py:41
  143.8 4.8 %fusion.10 = f32[512,2048]{1,0:T(8,128)S(1)} fusion(bf16[512,1024]{1,0:T(8,128)(2,1)} %all-gather.9.cloned.1.call-done, bf16[1024,2048]{1,0:T(8,128)(2,1)} %all-gather.11.cloned.1.call-done), kind=kOutput, calls=%fused_computation.20 | convolution fusion | flops 2147483648 | bytes 9437184 | tf_op jit(solution)/shard_map/dot_general | solution.py:46
  148.7 5.9 %multiply_convert_fusion = (bf16[512,2048]{1,0:T(8,128)(2,1)}, f32[512,2048]{1,0:T(8,128)}) fusion(f32[512,2048]{1,0:T(8,128)S(1)} %fusion.10, f32[512,128]{1,0:T(8,128)S(1)} %fusion.11, bf16[128,2048]{1,0:T(8,128)(2,1)S(1)} %copy-done), kind=kOutput, calls=%fused_computation.9 | convolution fusion | flops 1622147072 | bytes 11272192 | tf_op jit(solution)/shard_map/dot_general | solution.py:48
  154.6 69.7 %all-gather.7.cloned.1.call-done = bf16[2048,1024]{1,0:T(8,128)(2,1)} async-done(((bf16[2048,256]{1,0:T(8,128)(2,1)}), bf16[2048,1024]{1,0:T(8,128)(2,1)}) %all-gather.7.cloned.1.call-update) | async-done | bytes 4194320 | tf_op jit(solution)/shard_map/all_gather | solution.py:58
  224.3 4.7 %fusion.8 = f32[512,2048]{1,0:T(8,128)S(1)} fusion(bf16[512,1024]{1,0:T(8,128)(2,1)S(1)} %copy-done.3, bf16[2048,1024]{1,0:T(8,128)(2,1)} %all-gather.7.cloned.1.call-done), kind=kOutput, calls=%fused_computation.18 | convolution fusion | flops 2147483648 | bytes 9437184 | tf_op jit(solution)/shard_map/td,fd->tf/dot_general | solution.py:55
  229.1 5.1 %fusion.6 = bf16[512,2048]{1,0:T(8,128)(2,1)S(1)} fusion(f32[512,2048]{1,0:T(8,128)S(1)} %copy-done.8, f32[512,2048]{1,0:T(8,128)S(1)} %fusion.8, f32[512,128]{1,0:T(8,128)S(1)} %fusion.9, bf16[2048,128]{1,0:T(8,128)(2,1)S(1)} %copy-done.7), kind=kOutput, calls=%fused_computation.8 | convolution fusion | flops 1632632832 | bytes 11272192 | tf_op jit(solution)/shard_map/dot_general | solution.py:61
  234.1 0.7 fusion.13
  234.9 0.7 fusion.14
  235.6 0.7 fusion.16
  236.3 0.7 fusion.15
  236.9 1.1 pad_maximum_fusion
  238.0 0.0 all-reduce.3.cloned.1.call-start
  238.1 3.1 convolution_multiply_fusion.1
  241.2 3.3 convolution_multiply_fusion
  244.5 27.9 %reduce-scatter.5.cloned.1.call-done = f32[256,128]{1,0:T(8,128)} async-done(((f32[256,1024]{1,0:T(8,128)}), f32[256,128]{1,0:T(8,128)}) %reduce-scatter.5.cloned.1.call-update) | async-done | bytes 131088 | tf_op jit(solution)/shard_map/reduce_scatter | solution.py:84
  272.4 4.5 %fusion.12 = f32[512,1024]{1,0:T(8,128)S(1)} fusion(bf16[512,2048]{1,0:T(8,128)(2,1)S(1)} %fusion.6, bf16[1024,2048]{1,0:T(8,128)(2,1)} %all-gather.11.cloned.1.call-done), kind=kOutput, calls=%fused_computation.22 | convolution fusion | flops 2147483648 | bytes 8388608 | tf_op jit(solution)/shard_map/tf,df->td/dot_general | solution.py:68
  277.0 2.4 multiply_add_fusion.2
  279.4 86.5 %all-reduce.3.cloned.1.call-done = (f32[256,128]{1,0:T(8,128)}, f32[128,2048]{1,0:T(8,128)}, f32[2048,128]{1,0:T(8,128)}) async-done(((f32[256,128]{1,0:T(8,128)}, f32[128,2048]{1,0:T(8,128)}, f32[2048,128]{1,0:T(8,128)}), (f32[256,128]{1,0:T(8,128)}, f32[128,2048]{1,0:T(8,128)}, f32[2048,128]{1,0:T(8,128)})) %all-reduce.3.cloned.1.call-update) | async-done | bytes 2228240 | tf_op jit(solution)/shard_map/psum | solution.py:86
  365.8 1.5 slice_multiply_fusion
  367.4 0.7 copy.13
  368.1 41.8 %reduce-scatter.3.cloned.1.call-done = f32[512,128]{1,0:T(8,128)} async-done(((f32[512,1024]{1,0:T(8,128)}), f32[512,128]{1,0:T(8,128)}) %reduce-scatter.3.cloned.1.call-update) | async-done | bytes 262160 | tf_op jit(solution)/shard_map/reduce_scatter | solution.py:83
  409.9 2.3 copy.17
  412.2 2.3 copy.18
  (27 shorter events, 0.3 us)
Async XLA Ops:
  7.2 141.5 %copy-start = (bf16[128,2048]{1,0:T(8,128)(2,1)S(1)}, bf16[128,2048]{1,0:T(8,128)(2,1)}, u32[]{:S(2)}) copy-start(bf16[128,2048]{1,0:T(8,128)(2,1)} %param.13) | copy-start | bytes 1572868
  7.2 28.9 %all-gather.5.cloned.1.call-start = ((), (), s32[]{:S(2)}) async-start(), calls=%async_computation.2 | async-start | bytes 1179648 | tf_op jit(solution)/shard_map/all_gather | solution.py:39
  7.9 53.6 %all-gather.9.cloned.1.call-start = ((), (), s32[]{:S(2)}) async-start(), calls=%async_computation.4 | async-start | bytes 1179648 | tf_op jit(solution)/shard_map/all_gather | solution.py:38
  8.7 135.2 %all-gather.11.cloned.1.call-start = ((), (), s32[]{:S(2)}) async-start(), calls=%async_computation.5 | async-start | bytes 5242880 | tf_op jit(solution)/shard_map/all_gather | solution.py:41
  9.4 214.9 %all-gather.7.cloned.1.call-start = ((), (), s32[]{:S(2)}) async-start(), calls=%async_computation.3 | async-start | bytes 5242880 | tf_op jit(solution)/shard_map/all_gather | solution.py:58
  10.0 262.4 %reduce-scatter.5.cloned.1.call-start = ((), (), s32[]{:S(2)}) async-start(), calls=%async_computation.7 | async-start | bytes 1179648 | tf_op jit(solution)/shard_map/reduce_scatter | solution.py:84
  63.1 85.5 %copy-start.6 = (f32[512,128]{1,0:T(8,128)}, f32[512,128]{1,0:T(8,128)S(1)}, u32[]{:S(2)}) copy-start(f32[512,128]{1,0:T(8,128)S(1)} %fusion.11) | copy-start | bytes 786436
  148.7 75.6 %copy-start.3 = (bf16[512,1024]{1,0:T(8,128)(2,1)S(1)}, bf16[512,1024]{1,0:T(8,128)(2,1)}, u32[]{:S(2)}) copy-start(bf16[512,1024]{1,0:T(8,128)(2,1)} %all-gather.5.cloned.1.call-done) | copy-start | bytes 3145732
  224.3 4.7 %copy-start.7 = (bf16[2048,128]{1,0:T(8,128)(2,1)S(1)}, bf16[2048,128]{1,0:T(8,128)(2,1)}, u32[]{:S(2)}) copy-start(bf16[2048,128]{1,0:T(8,128)(2,1)} %param.14) | copy-start | bytes 1572868
  224.3 4.7 %copy-start.8 = (f32[512,2048]{1,0:T(8,128)S(1)}, f32[512,2048]{1,0:T(8,128)}, u32[]{:S(2)}) copy-start(f32[512,2048]{1,0:T(8,128)} %get-tuple-element.16) | copy-start | bytes 12582916
  229.0 5.8 %copy-start.1 = (bf16[512,2048]{1,0:T(8,128)(2,1)S(1)}, bf16[512,2048]{1,0:T(8,128)(2,1)}, u32[]{:S(2)}) copy-start(bf16[512,2048]{1,0:T(8,128)(2,1)} %get-tuple-element.15) | copy-start | bytes 6291460
  234.1 1.5 copy-start.5
  234.1 2.1 copy-start.4
  238.0 127.8 %all-reduce.3.cloned.1.call-start = ((), (), s32[]{:S(2)}) async-start(), calls=%async_computation.8 | async-start | bytes 4456448 | tf_op jit(solution)/shard_map/psum | solution.py:86
  238.1 3.1 copy-start.2
  272.4 137.5 %reduce-scatter.3.cloned.1.call-start = ((), (), s32[]{:S(2)}) async-start(), calls=%async_computation.6 | async-start | bytes 2359296 | tf_op jit(solution)/shard_map/reduce_scatter | solution.py:83
Sparse Core Ops, SparseCore 0:
  9.9 26.1 all-gather.4
  38.0 23.4 all-gather.8
  63.1 80.7 all-gather.10
  145.2 79.0 all-gather.6
  238.1 34.1 reduce-scatter.4
  275.4 90.4 all-reduce.2
  369.7 40.1 reduce-scatter.2
where the time goes:
time: 422 us; the launch traced here: 421 us
  waiting for transfers between devices  348 us (82%)
  matrix products  39.9 us (9%)
  between operations  14.3 us (3%)
  blocking collectives  11 us (3%)
  local copies, waits for them, and re-layouts  5.33 us (1%)
    psum x1, waiting for transfers between devices, local(): lax.psum((grad_out_a, grad_in_b, rank_local), 'tok')  86.5 us
    all_gather x1, waiting for transfers between devices, local(): in_rows = lax.all_gather(frozen_in, 'tok', axis=0, tiled=True)  80.7 us
    all_gather x1, waiting for transfers between devices, local(): lax.all_gather(frozen_out, 'tok', axis=1, tiled=True)  69.7 us
    reduce_scatter x1, waiting for transfers between devices, local(): lax.psum_scatter(dx_term, 'hid', scatter_dimension=1, tiled=True)  41.8 us
    reduce_scatter x1, waiting for transfers between devices, local(): lax.psum_scatter(rank_terms, 'hid', scatter_dimension=1, tiled=True)  27.9 us
    all_gather x1, waiting for transfers between devices, local(): lax.all_gather(tokens, 'hid', axis=1, tiled=True)  23.7 us
    all_gather x1, waiting for transfers between devices, local(): lax.all_gather(cotangent, 'hid', axis=1, tiled=True)  15.1 us
    all_gather x1, blocking collectives, local(): in_a_full = lax.all_gather(input_adapter_first, 'hid', axis=0, tiled=True)  11 us
  transfers between devices with their start and end apart: 7, of which 7 were waited for; matrix products, arithmetic and copies ran while one was open for 7% of the time, Pallas kernels for 0%

commit v1 on v0

--- a/solution.py
+++ b/solution.py
@@ -38,7 +38,12 @@
         lax.all_gather(tokens, "hid", axis=1, tiled=True),
         lax.all_gather(cotangent, "hid", axis=1, tiled=True),
     )
-    in_rows = lax.all_gather(frozen_in, "tok", axis=0, tiled=True)
+    ring = [frozen_in]
+    for hop in range(3):
+        ring.append(lax.ppermute(ring[-1], "tok", [(dev, (dev + 1) % 4) for dev in range(4)]))
+    in_rows = jnp.roll(
+        jnp.concatenate(ring[::-1], axis=0), (lax.axis_index("tok") + 1) * ring[0].shape[0], axis=0
+    )
     in_a_full = lax.all_gather(input_adapter_first, "hid", axis=0, tiled=True)
     lowrank_input = jnp.dot(full_tokens, in_a_full, preferred_element_type=jnp.float32)
     second_float = input_adapter_second.astype(jnp.float32)

time: 422 us -> 352 us (0.83)
  waiting for transfers between devices: 348 us -> 273 us
  local copies, waits for them, and re-layouts: 5.33 us -> 9.95 us
    all_gather x1 -> x0, waiting for transfers between devices: 80.7 us -> none  [local(): in_rows = lax.all_gather(frozen_in, 'tok', axis=0, tiled=True)]
    ppermute x0 -> x3, waiting for transfers between devices: none -> 76.4 us  [local(): lax.ppermute(ring[-1], 'tok', [(dev, (dev + 1) % 4) for dev in range(4)])]
    all_gather x1, waiting for transfers between devices: 69.7 us -> 40.1 us  [local(): lax.all_gather(frozen_out, 'tok', axis=1, tiled=True)]
    all_gather x1, waiting for transfers between devices: 23.7 us -> 0.01 us  [local(): lax.all_gather(tokens, 'hid', axis=1, tiled=True)]
    all_gather x1, waiting for transfers between devices: 15.1 us -> 0.02 us  [local(): lax.all_gather(cotangent, 'hid', axis=1, tiled=True)]
    unnamed x21 -> x32, local copies, waits for them, and re-layouts: 5.33 us -> 9.85 us
  transfers between devices with their start and end apart: 7 -> 9, of which waited for: 7 -> 7; matrix products, arithmetic and copies ran while one was open for 7% -> 9% of each run, Pallas kernels for 0% -> 0%
where the time goes in v1:
time: 352 us; the launch traced here: 351 us
  waiting for transfers between devices  273 us (78%)
  matrix products  38.9 us (11%)
  between operations  14.4 us (4%)
  local copies, waits for them, and re-layouts  9.95 us (3%)
  blocking collectives  9.29 us (3%)
    psum x1, waiting for transfers between devices, local(): lax.psum((grad_out_a, grad_in_b, rank_local), 'tok')  86.4 us
    ppermute x3, waiting for transfers between devices, local(): lax.ppermute(ring[-1], 'tok', [(dev, (dev + 1) % 4) for dev in range(4)])  76.4 us
    reduce_scatter x1, waiting for transfers between devices, local(): lax.psum_scatter(dx_term, 'hid', scatter_dimension=1, tiled=True)  41.7 us
    all_gather x1, waiting for transfers between devices, local(): lax.all_gather(frozen_out, 'tok', axis=1, tiled=True)  40.1 us
    reduce_scatter x1, waiting for transfers between devices, local(): lax.psum_scatter(rank_terms, 'hid', scatter_dimension=1, tiled=True)  26.9 us
    unnamed x32, local copies, waits for them, and re-layouts  9.85 us
    all_gather x1, blocking collectives, local(): in_a_full = lax.all_gather(input_adapter_first, 'hid', axis=0, tiled=True)  9.29 us
  transfers between devices with their start and end apart: 9, of which 7 were waited for; matrix products, arithmetic and copies ran while one was open for 9% of the time, Pallas kernels for 0%

profile of v1, /device:TPU:0, one launch (start us, length us, event | category | flops | bytes accessed | tf_op | source)
XLA Modules:
  0.0 351.4 jit_solution(11604966548931054688)
XLA Ops:
  7.2 0.7 all-gather.8.cloned.1.call-update
  8.0 0.7 all-gather.4.cloned.1.call-update
  8.7 3.1 collective-permute-start
  11.9 25.3 %collective-permute-done = bf16[256,2048]{1,0:T(8,128)(2,1)S(1)} collective-permute-done((bf16[256,2048]{1,0:T(8,128)(2,1)}, bf16[256,2048]{1,0:T(8,128)(2,1)S(1)}, u32[]{:S(2)}, u32[]{:S(2)}) %collective-permute-start) | collective-permute-done | bytes 1048608 | tf_op jit(solution)/shard_map/ppermute | solution.py:43
  37.2 26.1 %collective-permute-done.1 = bf16[256,2048]{1,0:T(8,128)(2,1)S(1)} collective-permute-done((bf16[256,2048]{1,0:T(8,128)(2,1)S(1)}, bf16[256,2048]{1,0:T(8,128)(2,1)S(1)}, u32[]{:S(2)}, u32[]{:S(2)}) %collective-permute-start.1) | collective-permute-done | bytes 1048608 | tf_op jit(solution)/shard_map/ppermute | solution.py:43
  63.3 9.3 %all_gather.15 = bf16[1024,128]{1,0:T(8,128)(2,1)S(1)} all-gather(bf16[128,128]{1,0:T(8,128)(2,1)} %param.12), channel_id=1, replica_groups=mesh['tok'=4,'hid'=8] {'hid'}, dimensions={0}, use_global_device_ids=true | all-gather | bytes 294912 | tf_op jit(solution)/shard_map/all_gather | solution.py:47
  72.6 1.7 fusion.20
  74.3 1.7 fusion.19
  76.1 2.9 fusion.21
  79.0 25.0 %collective-permute-done.2 = bf16[256,2048]{1,0:T(8,128)(2,1)} collective-permute-done((bf16[256,2048]{1,0:T(8,128)(2,1)S(1)}, bf16[256,2048]{1,0:T(8,128)(2,1)}, u32[]{:S(2)}, u32[]{:S(2)}) %collective-permute-start.2) | collective-permute-done | bytes 1048608 | tf_op jit(solution)/shard_map/ppermute | solution.py:43
  104.0 1.3 constant_dynamic-update-slice_fusion.7
  105.7 1.4 constant_dynamic-update-slice_fusion.3
  107.4 5.4 %multiply_convert_fusion = (bf16[512,2048]{1,0:T(8,128)(2,1)S(1)}, f32[512,2048]{1,0:T(8,128)}) fusion(f32[512,2048]{1,0:T(8,128)S(1)} %fusion.21, bf16[512,1024]{1,0:T(8,128)(2,1)S(1)} %copy-done.2, bf16[2048,2048]{1,0:T(8,128)(2,1)S(1)} %constant_dynamic-update-slice_fusion, s32[]{:T(128)S(6)} %select_n.14), kind=kOutput, calls=%fused_computation.10 | convolution fusion | flops 2159017984 | bytes 15728644 | tf_op jit(solution)/shard_map/dot_general | solution.py:51
  112.8 1.3 copy-done.1
  114.2 0.7 fusion.24
  114.9 1.4 fusion.25
  116.3 40.1 %all-gather.6.cloned.1.call-done = bf16[2048,1024]{1,0:T(8,128)(2,1)} async-done(((bf16[2048,256]{1,0:T(8,128)(2,1)}), bf16[2048,1024]{1,0:T(8,128)(2,1)}) %all-gather.6.cloned.1.call-update) | async-done | bytes 4194320 | tf_op jit(solution)/shard_map/all_gather | solution.py:63
  156.4 4.7 %fusion.18 = f32[512,2048]{1,0:T(8,128)S(1)} fusion(bf16[512,1024]{1,0:T(8,128)(2,1)S(1)} %copy-done.4, bf16[2048,1024]{1,0:T(8,128)(2,1)} %all-gather.6.cloned.1.call-done), kind=kOutput, calls=%fused_computation.32 | convolution fusion | flops 2147483648 | bytes 9437184 | tf_op jit(solution)/shard_map/td,fd->tf/dot_general | solution.py:60
  161.1 5.1 %fusion.6 = bf16[512,2048]{1,0:T(8,128)(2,1)S(1)} fusion(f32[512,2048]{1,0:T(8,128)S(1)} %copy-done.10, f32[512,2048]{1,0:T(8,128)S(1)} %fusion.18, f32[512,128]{1,0:T(8,128)S(1)} %fusion.19, bf16[2048,128]{1,0:T(8,128)(2,1)S(1)} %copy-done), kind=kOutput, calls=%fused_computation.8 | convolution fusion | flops 1632632832 | bytes 11272192 | tf_op jit(solution)/shard_map/dot_general | solution.py:66
  166.2 0.7 fusion.22
  167.6 1.0 pad_maximum_fusion
  168.8 4.9 %convolution_multiply_fusion = f32[2048,128]{1,0:T(8,128)} fusion(bf16[512,2048]{1,0:T(8,128)(2,1)} %copy-done.1, f32[512,128]{1,0:T(8,128)} %copy-done.8), kind=kOutput, calls=%fused_computation.15 | convolution fusion | flops 1610874880 | bytes 3407872 | tf_op jit(solution)/shard_map/dot_general | solution.py:74
  173.7 2.0 convolution_multiply_fusion.1
  175.7 26.9 %reduce-scatter.5.cloned.1.call-done = f32[256,128]{1,0:T(8,128)} async-done(((f32[256,1024]{1,0:T(8,128)}), f32[256,128]{1,0:T(8,128)}) %reduce-scatter.5.cloned.1.call-update) | async-done | bytes 131088 | tf_op jit(solution)/shard_map/reduce_scatter | solution.py:89
  202.7 1.0 fusion.23
  203.7 6.0 %multiply_add_fusion.1 = f32[512,1024]{1,0:T(8,128)} fusion(f32[512,1024]{1,0:T(8,128)S(1)} %fusion.23, bf16[512,2048]{1,0:T(8,128)(2,1)S(1)} %fusion.6, bf16[2048,2048]{1,0:T(8,128)(2,1)} %copy-done.9, s32[]{:T(128)S(6)} %select_n.14), kind=kOutput, calls=%fused_computation.17 | convolution fusion | flops 2148532224 | bytes 10485764 | tf_op jit(solution)/shard_map/tf,df->td/dot_general | solution.py:73
  209.7 86.4 %all-reduce.3.cloned.1.call-done = (f32[256,128]{1,0:T(8,128)}, f32[128,2048]{1,0:T(8,128)}, f32[2048,128]{1,0:T(8,128)}) async-done(((f32[256,128]{1,0:T(8,128)}, f32[128,2048]{1,0:T(8,128)}, f32[2048,128]{1,0:T(8,128)}), (f32[256,128]{1,0:T(8,128)}, f32[128,2048]{1,0:T(8,128)}, f32[2048,128]{1,0:T(8,128)})) %all-reduce.3.cloned.1.call-update) | async-done | bytes 2228240 | tf_op jit(solution)/shard_map/psum | solution.py:91
  296.1 1.5 slice_multiply_fusion
  297.6 0.7 copy.14
  298.4 41.7 %reduce-scatter.3.cloned.1.call-done = f32[512,128]{1,0:T(8,128)} async-done(((f32[512,1024]{1,0:T(8,128)}), f32[512,128]{1,0:T(8,128)}) %reduce-scatter.3.cloned.1.call-update) | async-done | bytes 262160 | tf_op jit(solution)/shard_map/reduce_scatter | solution.py:88
  340.0 2.3 copy.26
  342.3 2.3 copy.27
  (42 shorter events, 1.6 us)
Async XLA Ops:
  7.2 107.0 %copy-start = (bf16[2048,128]{1,0:T(8,128)(2,1)S(1)}, bf16[2048,128]{1,0:T(8,128)(2,1)}, u32[]{:S(2)}) copy-start(bf16[2048,128]{1,0:T(8,128)(2,1)} %param.14) | copy-start | bytes 1572868
  7.2 65.5 %all-gather.8.cloned.1.call-start = ((), (), s32[]{:S(2)}) async-start(), calls=%async_computation.4 | async-start | bytes 1179648 | tf_op jit(solution)/shard_map/all_gather | solution.py:38
  7.9 66.4 %all-gather.4.cloned.1.call-start = ((), (), s32[]{:S(2)}) async-start(), calls=%async_computation.2 | async-start | bytes 1179648 | tf_op jit(solution)/shard_map/all_gather | solution.py:39
  8.7 147.7 %all-gather.6.cloned.1.call-start = ((), (), s32[]{:S(2)}) async-start(), calls=%async_computation.3 | async-start | bytes 5242880 | tf_op jit(solution)/shard_map/all_gather | solution.py:63
  8.7 28.5 %collective-permute-start = (bf16[256,2048]{1,0:T(8,128)(2,1)}, bf16[256,2048]{1,0:T(8,128)(2,1)S(1)}, u32[]{:S(2)}, u32[]{:S(2)}) collective-permute-start(bf16[256,2048]{1,0:T(8,128)(2,1)} %param.10), channel_id=1, source_target_pairs={{0,8},{8,16},{16,24},{24,0},{1,9},{9,17},{17,25},{25,1},{2,10},{10... | collective-permute-start | bytes 3145736 | tf_op jit(solution)/shard_map/ppermute | solution.py:43
  11.8 190.8 %reduce-scatter.5.cloned.1.call-start = ((), (), s32[]{:S(2)}) async-start(), calls=%async_computation.6 | async-start | bytes 1179648 | tf_op jit(solution)/shard_map/reduce_scatter | solution.py:89
  37.2 26.1 %collective-permute-start.1 = (bf16[256,2048]{1,0:T(8,128)(2,1)S(1)}, bf16[256,2048]{1,0:T(8,128)(2,1)S(1)}, u32[]{:S(2)}, u32[]{:S(2)}) collective-permute-start(bf16[256,2048]{1,0:T(8,128)(2,1)S(1)} %collective-permute-done), channel_id=1, source_target_pairs={{0,8},{8,16},{16,24},{24,0},{1,9},{9,17},{17,25},{25,1},{2,10},{10... | collective-permute-start | bytes 3145736 | tf_op jit(solution)/shard_map/ppermute | solution.py:43
  63.3 40.7 %collective-permute-start.2 = (bf16[256,2048]{1,0:T(8,128)(2,1)S(1)}, bf16[256,2048]{1,0:T(8,128)(2,1)}, u32[]{:S(2)}, u32[]{:S(2)}) collective-permute-start(bf16[256,2048]{1,0:T(8,128)(2,1)S(1)} %collective-permute-done.1), channel_id=1, source_target_pairs={{0,8},{8,16},{16,24},{24,0},{1,9},{9,17},{17,25},{25,1},{2,10},{10... | collective-permute-start | bytes 3145736 | tf_op jit(solution)/shard_map/ppermute | solution.py:43
  76.1 85.0 %copy-start.8 = (f32[512,128]{1,0:T(8,128)}, f32[512,128]{1,0:T(8,128)S(1)}, u32[]{:S(2)}) copy-start(f32[512,128]{1,0:T(8,128)S(1)} %fusion.19) | copy-start | bytes 786436
  79.0 26.5 %copy-start.5 = (bf16[256,2048]{1,0:T(8,128)(2,1)S(1)}, bf16[256,2048]{1,0:T(8,128)(2,1)}, u32[]{:S(2)}) copy-start(bf16[256,2048]{1,0:T(8,128)(2,1)} %param.10) | copy-start | bytes 3145732
  105.7 1.7 copy-start.2
  107.4 5.4 %copy-start.9 = (bf16[2048,2048]{1,0:T(8,128)(2,1)}, bf16[2048,2048]{1,0:T(8,128)(2,1)S(1)}, u32[]{:S(2)}) copy-start(bf16[2048,2048]{1,0:T(8,128)(2,1)S(1)} %constant_dynamic-update-slice_fusion) | copy-start | bytes 25165828
  107.4 7.5 %copy-start.4 = (bf16[512,1024]{1,0:T(8,128)(2,1)S(1)}, bf16[512,1024]{1,0:T(8,128)(2,1)}, u32[]{:S(2)}) copy-start(bf16[512,1024]{1,0:T(8,128)(2,1)} %all-gather.4.cloned.1.call-done) | copy-start | bytes 3145732
  112.8 1.3 copy-start.1
  156.4 4.7 %copy-start.10 = (f32[512,2048]{1,0:T(8,128)S(1)}, f32[512,2048]{1,0:T(8,128)}, u32[]{:S(2)}) copy-start(f32[512,2048]{1,0:T(8,128)} %get-tuple-element.16) | copy-start | bytes 12582916
  161.1 5.1 %copy-start.6 = (bf16[128,2048]{1,0:T(8,128)(2,1)S(1)}, bf16[128,2048]{1,0:T(8,128)(2,1)}, u32[]{:S(2)}) copy-start(bf16[128,2048]{1,0:T(8,128)(2,1)} %param.13) | copy-start | bytes 1572868
  161.1 5.8 %copy-start.3 = (bf16[512,1024]{1,0:T(8,128)(2,1)S(1)}, bf16[512,1024]{1,0:T(8,128)(2,1)}, u32[]{:S(2)}) copy-start(bf16[512,1024]{1,0:T(8,128)(2,1)} %all-gather.8.cloned.1.call-done) | copy-start | bytes 3145732
  166.2 1.4 copy-start.7
  168.7 127.4 %all-reduce.3.cloned.1.call-start = ((), (), s32[]{:S(2)}) async-start(), calls=%async_computation.7 | async-start | bytes 4456448 | tf_op jit(solution)/shard_map/psum | solution.py:91
  202.6 137.4 %reduce-scatter.3.cloned.1.call-start = ((), (), s32[]{:S(2)}) async-start(), calls=%async_computation.5 | async-start | bytes 2359296 | tf_op jit(solution)/shard_map/reduce_scatter | solution.py:88
Sparse Core Ops, SparseCore 0:
  9.9 26.1 all-gather.7
  38.0 23.4 all-gather.3
  63.1 93.2 all-gather.5
  168.8 33.7 reduce-scatter.4
  205.6 90.4 all-reduce.2
  299.8 40.1 reduce-scatter.2
